TPU v7x, 256 devices: a whole 4x4x8 slice. The times are simulated.
256 devices in a mesh: tm: 4 (over x), area: 64 (over z, y, core).
Axes of the slice: x: 4, y: 4, z: 8, core: 2. Of those that a mesh axis runs over, the one named last changes fastest.
Arguments:
- gradient: float32 [168, 256, 512], P('tm', 'area'), may hold values from -72 to 72
- barrier: float32 [1], replicated, may hold values from 0.5 to 2
- slack: float32 [168, 256, 512], P('tm', 'area'), may hold values from 0.5 to 2
- hess_diag: float32 [168, 256, 512], P('tm', 'area'), may hold values from 0.5 to 2
- tile: float32 [256, 512, 512], P('area'), may hold values from -0.1 to 4.1, as said below
- ramp_weight: float32 [256, 512], P('area'), may hold values from 0.5 to 2
- bus_coupling: float32 [256, 512], P('area'), may hold values from 0.5 to 2
- tie_offset: int32 [256, 4], replicated, may hold values from 1 to 4, as said below
- tie_admittance: float32 [256, 4], replicated, may hold values from 0.5 to 2
- con_sens: float32 [16384, 512], P('area'), may hold values from -0.9 to 0.9
- con_weight: float32 [16384, 168], P('area', 'tm'), may hold values from 0.5 to 2
- con_owner: int32 [16384, 1], P('area'), may hold values from 0 to 255; in each aligned block of 256 rows (0 to 255, 256 to 511, ...) at most 2 rows name the same one
- step_guess: float32 [168, 256, 512], P('tm', 'area'), may hold values from -1.2 to 1.2
Outputs:
- newton_step: float32 [168, 256, 512], P('tm', 'area')
- residual: float32 [168, 256, 512], P('tm', 'area')
Inputs may be any that keep to these rules, and one draw needn't show every extreme that they name: `tie_offset`: each tie partner lies 1 to 4 areas above its area; a partner past the last area is absent. `con_owner`: on the rows of one index of area, no area owns more than 2 blocks. Each area's tile is symmetric.
All inputs are finite; a program needn't handle non-finite values.
Results may differ from a plain program's by a relative error of at most 0.00028.
Values sent between devices are 32-bit elements; how exact they have to be, the bound alone decides.
A program may use at most 64 MiB of HBM per device.

v0:
```python
import functools

import jax
import jax.numpy as jnp
from jax import lax
from jax.experimental import pallas as pl
from jax.experimental.pallas import tpu as pltpu
from jax.sharding import PartitionSpec as P

MESH = pl.DeviceIdType.MESH
TIES = 4
HOUR_TILE = 8
Y_SIZE = 4
CORES = 2
F32 = jnp.float32
BF16 = jnp.bfloat16


def split(x):
    high = x.astype(BF16)
    return high, (x - high.astype(F32)).astype(BF16)


def product(stacked, high, right_high, right_low, dims):
    rows = high.shape[0]
    first = lax.dot_general(stacked, right_high, dims, preferred_element_type=F32)
    second = lax.dot_general(high, right_low, dims, preferred_element_type=F32)
    return first[:rows] + first[rows:] + second


NN = (((1,), (0,)), ((), ()))
NT = (((1,), (1,)), ((), ()))


def lane_sum(x):
    row = jnp.sum(x, axis=0, keepdims=True)
    width = row.shape[1]
    total = row[:, 0:128]
    for start in range(128, width, 128):
        total = total + row[:, start : start + 128]
    return total


def kernel(
    hours, tm_size, area_size,
    tie_window, diag_ref, right_ref, guess_ref, tile_hbm, ramp_ref, coup_ref, sens_hbm, weight_ref,
    step_ref, resid_ref,
    tile_buf, tile_high, tile_low, sens_buf, sens_high, sens_low,
    diag_buf, tie_buf, field, acc, halo, hour_stage, hour_halo, coup_halo,
    red_stage, red_slots,
    load_sem, halo_send, halo_recv, hour_send, hour_recv, coup_send, coup_recv, red_send, red_recv,
):
    span = guess_ref.shape[0]
    padded = guess_ref.shape[1]
    width = guess_ref.shape[2]
    me_t = lax.axis_index("tm")
    me_a = lax.axis_index("area")
    zed = lax.div(me_a, Y_SIZE * CORES)
    wye = lax.rem(lax.div(me_a, CORES), Y_SIZE)
    core = lax.rem(me_a, CORES)
    count_one = tm_size * Y_SIZE
    count_two = area_size // Y_SIZE
    mine = (me_t * Y_SIZE + wye, zed * CORES + core)
    counts = (count_one, count_two)

    def partner(stage, index):
        if stage == 0:
            t = lax.div(index, Y_SIZE)
            y = lax.rem(index, Y_SIZE)
            return (t, zed * (Y_SIZE * CORES) + y * CORES + core)
        z = lax.div(index, CORES)
        c = lax.rem(index, CORES)
        return (me_t, z * (Y_SIZE * CORES) + wye * CORES + c)

    above = (me_t, lax.rem(me_a + 1, area_size))
    below = (me_t, lax.rem(me_a + area_size - 1, area_size))
    later = (lax.rem(me_t + 1, tm_size), me_a)
    earlier = (lax.rem(me_t + tm_size - 1, tm_size), me_a)

    tile_load = pltpu.make_async_copy(tile_hbm, tile_buf, load_sem.at[0])
    tile_load.start()
    sens_load = pltpu.make_async_copy(sens_hbm, sens_buf, load_sem.at[1])
    sens_load.start()

    barrier = pltpu.get_barrier_semaphore()
    greeted = 0
    for stage in range(2):
        for d in range(1, counts[stage]):
            other = partner(stage, lax.rem(mine[stage] + d, counts[stage]))
            pl.semaphore_signal(barrier, inc=1, device_id=other, device_id_type=MESH)
            greeted += 1
    for other in (above, below):
        pl.semaphore_signal(barrier, inc=1, device_id=other, device_id_type=MESH)
        greeted += 1

    def stage_hours(phase, source):
        for i in range(span):
            hour_stage[phase, 0, i : i + 1, :] = source[i, 0:1, :]
            hour_stage[phase, 1, i : i + 1, :] = source[i, hours - 1 : hours, :]

    stage_hours(0, guess_ref)
    pl.semaphore_wait(barrier, greeted)

    def remote(source, target, send, recv, device):
        return pltpu.make_async_remote_copy(
            src_ref=source, dst_ref=target, send_sem=send, recv_sem=recv,
            device_id=device, device_id_type=MESH,
        )

    coup_copies = [
        remote(coup_ref, coup_halo.at[0], coup_send.at[0], coup_recv.at[0], above),
        remote(coup_ref, coup_halo.at[1], coup_send.at[1], coup_recv.at[1], below),
    ]
    for copy in coup_copies:
        copy.start()

    def field_copies(phase, source, i):
        return [
            remote(source.at[i], halo.at[phase, 0, i], halo_send.at[phase, 0, i], halo_recv.at[phase, 0, i], above),
            remote(source.at[i], halo.at[phase, 1, i], halo_send.at[phase, 1, i], halo_recv.at[phase, 1, i], below),
        ]

    def hour_copies(phase):
        return [
            remote(hour_stage.at[phase, 1], hour_halo.at[phase, 0], hour_send.at[phase, 0], hour_recv.at[phase, 0], later),
            remote(hour_stage.at[phase, 0], hour_halo.at[phase, 1], hour_send.at[phase, 1], hour_recv.at[phase, 1], earlier),
        ]

    flying = [[], [], []]
    for i in range(span):
        flying[0] += field_copies(0, guess_ref, i)
    flying[0] += hour_copies(0)
    for copy in flying[0]:
        copy.start()

    tile_load.wait()
    for i in range(span):
        high, low = split(tile_buf[i])
        tile_high[i] = high
        tile_low[i] = low
    sens_load.wait()
    for i in range(span):
        high, low = split(sens_buf[i])
        sens_high[i] = high
        sens_low[i] = low

    for copy in coup_copies:
        copy.wait()
    coupling = [coup_halo[0, i : i + 1, :] for i in range(span)]
    coupling += [coup_ref[i : i + 1, :] for i in range(span)]
    coupling += [coup_halo[1, i : i + 1, :] for i in range(span)]
    offsets = [o for o in range(-TIES, TIES + 1) if o != 0]
    for i in range(span):
        total = 2.0 * ramp_ref[i : i + 1, :]
        for k, o in enumerate(offsets):
            gain = tie_window[span + i, o - 1] if o > 0 else tie_window[span + i + o, -o - 1]
            row = coupling[span + i] * coupling[span + i + o] * gain
            tie_buf[i, k : k + 1, :] = row
            total = total + row
        diag_buf[i] = diag_ref[i] + total

    def local_part(value, i):
        high, low = split(value)
        stacked = jnp.concatenate([high, low], axis=0)
        result = product(stacked, high, tile_high[i], tile_low[i], NN)
        flow = product(stacked, high, sens_high[i], sens_low[i], NT) * weight_ref[i]
        flow_high, flow_low = split(flow)
        flow_stacked = jnp.concatenate([flow_high, flow_low], axis=0)
        return result + product(flow_stacked, flow_high, sens_high[i], sens_low[i], NN)

    rows = lax.broadcasted_iota(jnp.int32, (padded, width), 0)
    first_hours = me_t == 0
    last_hours = me_t == tm_size - 1

    def finish(phase, source, i):
        value = source[i]
        before = hour_halo[phase, 0, i : i + 1, :]
        before = jnp.where(first_hours, jnp.zeros_like(before), before)
        after = hour_halo[phase, 1, i : i + 1, :]
        after = jnp.where(last_hours, jnp.zeros_like(after), after)
        up = jnp.where(rows == hours - 1, after, pltpu.roll(value, padded - 1, 0))
        down = jnp.where(rows == 0, before, pltpu.roll(value, 1, 0))
        out = acc[i] + diag_buf[i] * value - ramp_ref[i : i + 1, :] * (up + down)
        for k, o in enumerate(offsets):
            j = i + o
            if j < 0:
                near = halo[phase, 0, span + j]
            elif j < span:
                near = source[j]
            else:
                near = halo[phase, 1, j - span]
            out = out - tie_buf[i, k : k + 1, :] * near
        return jnp.where(rows < hours, out, jnp.zeros_like(out))

    def start_stage(which, stage):
        copies = []
        for d in range(1, counts[stage]):
            to = lax.rem(mine[stage] + d, counts[stage])
            copy = remote(
                red_stage.at[which, stage], red_slots.at[which, stage, mine[stage]],
                red_send.at[which, stage, d], red_recv.at[which, stage, d], partner(stage, to),
            )
            copy.start()
            copies.append(copy)
        return copies

    def end_stage(which, stage, copies):
        for copy in copies:
            copy.wait()
        total = jnp.zeros((8, 128), F32)
        for s in range(counts[stage]):
            total = total + red_slots[which, stage, s]
        return total

    def begin(which, stage, tile):
        red_stage[which, stage] = tile
        red_slots[which, stage, mine[stage]] = tile
        return start_stage(which, stage)

    def pack(values):
        filled = jnp.zeros((8 - len(values), 128), F32)
        return jnp.concatenate(values + [filled], axis=0)

    def send_phase(phase, source):
        copies = []
        for i in range(span):
            copies += field_copies(phase, source, i)
        stage_hours(phase, source)
        copies += hour_copies(phase)
        for copy in copies:
            copy.start()
        flying[phase] = copies

    for i in range(span):
        acc[i] = local_part(guess_ref[i], i)
    for copy in flying[0]:
        copy.wait()
    sum_rr = jnp.zeros((1, 128), F32)
    for i in range(span):
        value = right_ref[i] - finish(0, guess_ref, i)
        field[0, i] = value
        sum_rr = sum_rr + lane_sum(value * value)
    send_phase(1, field.at[0])
    for i in range(span):
        acc[i] = local_part(field[0, i], i)
    for copy in flying[1]:
        copy.wait()
    sum_rv = jnp.zeros((1, 128), F32)
    for i in range(span):
        value = finish(1, field.at[0], i)
        field[1, i] = value
        sum_rv = sum_rv + lane_sum(value * field[0, i])
    send_phase(2, field.at[1])
    copies = begin(0, 0, pack([sum_rr, sum_rv]))
    half = span // 2
    for i in range(half):
        acc[i] = local_part(field[1, i], i)
    total = end_stage(0, 0, copies)
    copies = begin(0, 1, total)
    for i in range(half, span):
        acc[i] = local_part(field[1, i], i)
    for copy in flying[2]:
        copy.wait()
    for i in range(span):
        field[2, i] = finish(2, field.at[1], i)
    total = jnp.sum(end_stage(0, 1, copies), axis=1, keepdims=True)
    rr_zero, rv_zero = total[0:1], total[1:2]
    alpha_zero = rr_zero / rv_zero

    sums = [jnp.zeros((1, 128), F32) for _ in range(4)]
    for i in range(span):
        zero, one, two = field[0, i], field[1, i], field[2, i]
        resid = zero - alpha_zero * one
        image = one - alpha_zero * two
        field[2, i] = image
        acc[i] = resid
        sums[0] = sums[0] + lane_sum(resid * resid)
        sums[1] = sums[1] + lane_sum(resid * image)
        sums[2] = sums[2] + lane_sum(resid * one)
        sums[3] = sums[3] + lane_sum(zero * image)
    copies = begin(1, 0, pack(sums))
    total = end_stage(1, 0, copies)
    copies = begin(1, 1, total)
    total = jnp.sum(end_stage(1, 1, copies), axis=1, keepdims=True)
    beta = total[0:1] / rr_zero
    bend = total[1:2] + beta * (total[2:3] + total[3:4]) + beta * beta * rv_zero
    alpha_one = total[0:1] / bend
    for i in range(span):
        resid = acc[i]
        zero = field[0, i]
        step_ref[i] = guess_ref[i] + alpha_zero * zero + alpha_one * (resid + beta * zero)
        resid_ref[i] = resid - alpha_one * (field[2, i] + beta * field[1, i])


def newton_kernel(tie_window, diag, right, guess, tile, ramp, coup, sens, weight, hours, tm_size, area_size):
    span, padded, width = guess.shape
    slots = sens.shape[1]
    most = max(tm_size * Y_SIZE, area_size // Y_SIZE)
    vmem = pl.BlockSpec(memory_space=pltpu.VMEM)
    anywhere = pl.BlockSpec(memory_space=pl.ANY)
    dma = pltpu.SemaphoreType.DMA
    shape = jax.ShapeDtypeStruct(guess.shape, F32)
    return pl.pallas_call(
        functools.partial(kernel, hours, tm_size, area_size),
        out_shape=(shape, shape),
        in_specs=[pl.BlockSpec(memory_space=pltpu.SMEM), vmem, vmem, vmem, anywhere, vmem, vmem, anywhere, vmem],
        out_specs=(vmem, vmem),
        scratch_shapes=[
            pltpu.VMEM(tile.shape, F32), pltpu.VMEM(tile.shape, BF16), pltpu.VMEM(tile.shape, BF16),
            pltpu.VMEM(sens.shape, F32), pltpu.VMEM(sens.shape, BF16), pltpu.VMEM(sens.shape, BF16),
            pltpu.VMEM(guess.shape, F32),
            pltpu.VMEM((span, 2 * TIES, width), F32),
            pltpu.VMEM((3,) + guess.shape, F32),
            pltpu.VMEM(guess.shape, F32),
            pltpu.VMEM((3, 2) + guess.shape, F32),
            pltpu.VMEM((3, 2, span, width), F32),
            pltpu.VMEM((3, 2, span, width), F32),
            pltpu.VMEM((2, span, width), F32),
            pltpu.VMEM((2, 2, 8, 128), F32),
            pltpu.VMEM((2, 2, most, 8, 128), F32),
            dma((2,)), dma((3, 2, span)), dma((3, 2, span)), dma((3, 2)), dma((3, 2)), dma((2,)), dma((2,)),
            dma((2, 2, most)), dma((2, 2, most)),
        ],
        compiler_params=pltpu.CompilerParams(collective_id=0, has_side_effects=True, vmem_limit_bytes=60 * 1024 * 1024),
    )(tie_window, diag, right, guess, tile, ramp, coup, sens, weight)


def body(
    gradient, barrier, slack, hess_diag, tile, ramp_weight, bus_coupling, tie_offset, tie_admittance,
    con_sens, con_weight, con_owner, step_guess,
):
    hour_count, span_areas, var_width = gradient.shape
    area_total = tie_offset.shape[0]
    groups = lax.axis_size("area")
    first_area = lax.axis_index("area") * span_areas
    capacity = max(2, (2 * con_sens.shape[0] + area_total - 1) // area_total)
    owner_area = con_owner[:, 0]
    owner_marks = (owner_area[:, None] == jnp.arange(area_total, dtype=jnp.int32)[None, :]).astype(jnp.int32)
    before = jnp.cumsum(owner_marks, axis=0) - owner_marks
    slot_rank = jnp.sum(before * owner_marks, axis=1)
    slot_index = owner_area * capacity + slot_rank
    send_sens = jnp.zeros((area_total * capacity, var_width), F32).at[slot_index].set(con_sens)
    send_weight = jnp.zeros((area_total * capacity, hour_count), F32).at[slot_index].set(con_weight)
    send_sens = send_sens.reshape(groups, span_areas * capacity, var_width)
    send_weight = send_weight.reshape(groups, span_areas * capacity, hour_count)
    got_sens = lax.all_to_all(send_sens, "area", split_axis=0, concat_axis=0, tiled=True)
    got_weight = lax.all_to_all(send_weight, "area", split_axis=0, concat_axis=0, tiled=True)
    padded = -(-hour_count // HOUR_TILE) * HOUR_TILE
    fill = ((0, 0), (0, padded - hour_count), (0, 0))
    slots = groups * capacity
    owned_sens = jnp.transpose(
        got_sens.reshape(groups, span_areas, capacity, var_width), (1, 0, 2, 3)
    ).reshape(span_areas, slots, var_width)
    owned_weight = jnp.transpose(
        got_weight.reshape(groups, span_areas, capacity, hour_count), (1, 3, 0, 2)
    ).reshape(span_areas, hour_count, slots)
    owned_weight = jnp.pad(owned_weight, fill)

    def by_area(x):
        return jnp.pad(jnp.transpose(x, (1, 0, 2)), fill)

    diag = by_area(hess_diag + barrier[0] / (slack * slack))
    right = by_area(barrier[0] / slack - gradient)
    guess = by_area(step_guess)

    reach = jnp.arange(1, TIES + 1, dtype=jnp.int32)
    inside = (jnp.arange(area_total, dtype=jnp.int32)[:, None] + reach[None, :]) < area_total
    gains = jnp.sum(
        jnp.where(tie_offset[:, :, None] == reach[None, None, :], tie_admittance[:, :, None], 0.0), axis=1
    )
    gains = jnp.where(inside, gains, 0.0)
    gains = jnp.concatenate([jnp.zeros((span_areas, TIES), F32), gains], axis=0)
    tie_window = lax.dynamic_slice(gains, (first_area, jnp.int32(0)), (2 * span_areas, TIES))

    step, residual = newton_kernel(
        tie_window, diag, right, guess, tile, ramp_weight, bus_coupling, owned_sens, owned_weight,
        hour_count, lax.axis_size("tm"), groups,
    )
    return (
        jnp.transpose(step[:, :hour_count], (1, 0, 2)),
        jnp.transpose(residual[:, :hour_count], (1, 0, 2)),
    )


def solution(mesh):
    placed = (
        P("tm", "area", None), P(), P("tm", "area", None), P("tm", "area", None), P("area", None, None),
        P("area", None), P("area", None), P(), P(), P("area", None), P("area", "tm"), P("area", None),
        P("tm", "area", None),
    )
    return jax.shard_map(
        body, mesh=mesh, in_specs=placed,
        out_specs=(P("tm", "area", None), P("tm", "area", None)), check_vma=False,
    )
```

profile of v0, /device:TPU:1, one launch (start us, length us, event | category | flops | bytes accessed | tf_op | source)
XLA Modules:
  0.0 117.2 jit_solution(10396460403412478754)
XLA Ops:
  0.6 0.0 copy-start.5
  0.6 0.0 copy-start.4
  0.7 0.0 copy-start.1
  0.7 0.0 copy-start
  0.7 0.0 copy-start.2
  0.7 0.9 copy.88
  1.6 0.2 fusion.7
  1.8 0.0 copy-start.3
  1.9 0.9 fusion.9
  2.8 0.7 compare_select_fusion
  3.5 0.9 copy.92
  4.4 1.2 %scatter_custom_fusion.1 = f32[512,42]{1,0:T(8,128)S(1)} fusion(s32[256]{0:T(256)S(1)} %bitcast.50, f32[256,42]{1,0:T(8,128)S(1)} %copy.92, f32[]{:T(128)} %constant.11.clone.1), kind=kCustom, calls=%fused_computation.22 | custom fusion | bytes 86020 | tf_op jit(solution)/shard_map/scatter | solution.py:343
  5.6 0.9 reshape.76
  6.5 13.1 %all-to-all-start.1 = ((f32[64,1,336]{2,1,0:T(1,128)}), f32[64,1,336]{2,1,0:T(1,128)S(1)}, u32[]{:S(2)}, u32[]{:S(2)}) async-start(f32[64,1,336]{2,1,0:T(1,128)} %reshape.76), calls=%async_computation.1 | async-start | bytes 196608 | tf_op jit(solution)/shard_map/all_to_all | solution.py:347
  19.7 2.9 %scatter_custom_fusion = f32[512,512]{1,0:T(8,128)} fusion(s32[256]{0:T(256)S(1)} %bitcast.51, f32[256,512]{1,0:T(8,128)} %param.22, f32[]{:T(128)} %constant.11.clone.1), kind=kCustom, calls=%fused_computation.2 | custom fusion | bytes 1049088 | tf_op jit(solution)/shard_map/scatter | solution.py:342
  22.6 7.7 %all-to-all-done.1 = f32[64,1,336]{2,1,0:T(1,128)S(1)} async-done(((f32[64,1,336]{2,1,0:T(1,128)}), f32[64,1,336]{2,1,0:T(1,128)S(1)}, u32[]{:S(2)}, u32[]{:S(2)}) %all-to-all-start.1) | async-done | bytes 86048 | tf_op jit(solution)/shard_map/all_to_all | solution.py:347
  30.2 4.5 %all-to-all-start = ((f32[64,8,512]{2,1,0:T(8,128)}), f32[64,8,512]{2,1,0:T(8,128)S(1)}, u32[]{:S(2)}, u32[]{:S(2)}) async-start(f32[64,8,512]{2,1,0:T(8,128)} %bitcast.11), calls=%async_computation | async-start | bytes 2097152 | tf_op jit(solution)/shard_map/all_to_all | solution.py:346
  34.8 0.0 copy-done.5
  34.8 0.0 copy-done.4
  34.8 0.1 select_reduce_fusion
  34.9 0.1 copy.81
  35.7 0.0 copy-done.1
  35.7 0.0 copy-done
  35.7 0.0 copy-done.2
  35.7 0.3 fusion.6
  36.0 0.8 pad.15.diag_ref
  36.8 0.8 pad.16.right_ref
  37.6 0.0 copy-done.3
  37.6 0.1 copy.113
  37.7 0.8 pad.17.guess_ref
  38.5 0.6 pad_dynamic-slice_fusion.tie_window
  39.1 0.5 broadcast.58
  39.6 0.9 reduce
  40.5 0.1 reshape.77
  40.6 0.2 copy.93
  40.8 0.2 copy.94
  41.0 0.1 copy.95
  41.1 0.7 pad.18.weight_ref
  41.8 21.2 %all-to-all-done = f32[64,8,512]{2,1,0:T(8,128)S(1)} async-done(((f32[64,8,512]{2,1,0:T(8,128)}), f32[64,8,512]{2,1,0:T(8,128)S(1)}, u32[]{:S(2)}, u32[]{:S(2)}) %all-to-all-start) | async-done | bytes 1048608 | tf_op jit(solution)/shard_map/all_to_all | solution.py:346
  63.0 0.6 copy.90
  63.7 0.8 copy.91
  64.5 1.7 %reshape.52.sens_hbm = f32[4,128,512]{2,1,0:T(8,128)} reshape(f32[4,64,2,512]{3,2,1,0:T(2,128)S(1)} %copy.91) | data formatting | bytes 2097152 | tf_op jit(solution)/shard_map/reshape | solution.py:353
  66.2 47.9 %shard_map.140 = (f32[4,48,512]{2,1,0:T(8,128)}, f32[4,48,512]{2,1,0:T(8,128)}) custom-call(f32[8,4]{1,0:T(8,128)} %pad_dynamic-slice_fusion.tie_window, f32[4,48,512]{2,1,0:T(8,128)} %pad.15.diag_ref, f32[4,48,512]{2,1,0:T(8,128)} %pad.16.right_ref, f32[4,48,512]{2,1,0:T(8,128)} %pad.17.guess_ref, f32[4,512,512]{2,1,0:T(8,128)} %tile_hbm.1, ...), custom_call_target="tpu_custom_call" | custom-call | tf_op jit(solution)/shard_map/pallas_call | solution.py:303
  114.1 1.2 %slice_bitcast_fusion = (f32[42,4,512]{2,0,1:T(8,128)S(1)}, f32[42,4,512]{2,0,1:T(8,128)S(1)}) fusion(f32[4,48,512]{2,1,0:T(8,128)} %get-tuple-element.5, f32[4,48,512]{2,1,0:T(8,128)} %get-tuple-element.4), kind=kLoop, calls=%fused_computation.13 | loop fusion | bytes 1376256 | tf_op jit(solution)/shard_map/transpose | solution.py:381
  115.3 1.0 copy.96
  116.3 1.0 copy.97
  (8 shorter events, 0.1 us)
Async XLA Ops:
  0.6 34.1 %copy-start.5 = (s32[256,4]{0,1:T(4,128)S(1)}, s32[256,4]{0,1:T(4,128)}, u32[]{:S(2)}) copy-start(s32[256,4]{0,1:T(4,128)} %param.20) | copy-start | bytes 12292
  0.6 34.1 %copy-start.4 = (f32[256,4]{0,1:T(4,128)S(1)}, f32[256,4]{0,1:T(4,128)}, u32[]{:S(2)}) copy-start(f32[256,4]{0,1:T(4,128)} %param.21) | copy-start | bytes 12292
  0.7 35.0 %copy-start.1 = (f32[42,4,512]{2,1,0:T(4,128)S(1)}, f32[42,4,512]{2,1,0:T(4,128)}, u32[]{:S(2)}) copy-start(f32[42,4,512]{2,1,0:T(4,128)} %param.13) | copy-start | bytes 1032196
  0.7 35.0 %copy-start = (f32[42,4,512]{2,1,0:T(4,128)S(1)}, f32[42,4,512]{2,1,0:T(4,128)}, u32[]{:S(2)}) copy-start(f32[42,4,512]{2,1,0:T(4,128)} %param.15) | copy-start | bytes 1032196
  0.7 35.0 %copy-start.2 = (f32[42,4,512]{2,1,0:T(4,128)S(1)}, f32[42,4,512]{2,1,0:T(4,128)}, u32[]{:S(2)}) copy-start(f32[42,4,512]{2,1,0:T(4,128)} %param.16) | copy-start | bytes 1032196
  1.8 35.7 %copy-start.3 = (f32[42,4,512]{2,1,0:T(4,128)S(1)}, f32[42,4,512]{2,1,0:T(4,128)}, u32[]{:S(2)}) copy-start(f32[42,4,512]{2,1,0:T(4,128)} %param.25) | copy-start | bytes 1032196
  6.5 23.7 %all-to-all-start.1 = ((f32[64,1,336]{2,1,0:T(1,128)}), f32[64,1,336]{2,1,0:T(1,128)S(1)}, u32[]{:S(2)}, u32[]{:S(2)}) async-start(f32[64,1,336]{2,1,0:T(1,128)} %reshape.76), calls=%async_computation.1 | async-start | bytes 196608 | tf_op jit(solution)/shard_map/all_to_all | solution.py:347
  30.2 32.8 %all-to-all-start = ((f32[64,8,512]{2,1,0:T(8,128)}), f32[64,8,512]{2,1,0:T(8,128)S(1)}, u32[]{:S(2)}, u32[]{:S(2)}) async-start(f32[64,8,512]{2,1,0:T(8,128)} %bitcast.11), calls=%async_computation | async-start | bytes 2097152 | tf_op jit(solution)/shard_map/all_to_all | solution.py:346
where the time goes:
time: 118 us; the launch traced here: 117 us
  Pallas kernels  47.9 us (41%)
  waiting for transfers between devices  28.9 us (24%)
  local copies, waits for them, and re-layouts  18.1 us (15%)
  starting transfers between devices  17.6 us (15%)
  other arithmetic  3.15 us (3%)
  between operations  1.52 us (1%)
    pallas_call x1, Pallas kernels, newton_kernel(): pl.pallas_call(functools.partial(kernel, hours, tm_size, area_size), out_...  47.9 us
    all_to_all x1, waiting for transfers between devices, body(): lax.all_to_all(send_sens, 'area', split_axis=0, concat_axis=0, tiled=True)  21.2 us
    all_to_all x1, starting transfers between devices, body(): lax.all_to_all(send_weight, 'area', split_axis=0, concat_axis=0, tiled=True)  13.1 us
    all_to_all x1, waiting for transfers between devices, body(): lax.all_to_all(send_weight, 'area', split_axis=0, concat_axis=0, tiled=True)  7.66 us
    all_to_all x1, starting transfers between devices, body(): lax.all_to_all(send_sens, 'area', split_axis=0, concat_axis=0, tiled=True)  4.49 us
    unnamed x19, local copies, waits for them, and re-layouts  3.98 us
    scatter x1, local copies, waits for them, and re-layouts, body(): jnp.zeros((area_total * capacity, var_width), F32).at[slot_index]  2.93 us
  transfers between devices with their start and end apart: 2, of which 2 were waited for; matrix products, arithmetic and copies ran while one was open for 8% of the time, Pallas kernels for 0%

commit v1 on v0

v1 whole, which is shorter than its diff:
```python
import functools

import jax
import jax.numpy as jnp
from jax import lax
from jax.experimental import pallas as pl
from jax.experimental.pallas import tpu as pltpu
from jax.sharding import PartitionSpec as P

MESH = pl.DeviceIdType.MESH
TIES = 4
CAPACITY = 2
Y_SIZE = 4
CORES = 2
F32 = jnp.float32
BF16 = jnp.bfloat16


def split(x):
    high = x.astype(BF16)
    return high, (x - high.astype(F32)).astype(BF16)


def product(stacked, high, right_high, right_low, dims):
    rows = high.shape[0]
    first = lax.dot_general(stacked, right_high, dims, preferred_element_type=F32)
    second = lax.dot_general(high, right_low, dims, preferred_element_type=F32)
    return first[:rows] + first[rows:] + second


NN = (((1,), (0,)), ((), ()))
NT = (((1,), (1,)), ((), ()))


def lane_sum(x):
    row = jnp.sum(x, axis=0, keepdims=True)
    width = row.shape[1]
    total = row[:, 0:128]
    for start in range(128, width, 128):
        total = total + row[:, start : start + 128]
    return total


def kernel(
    hours, tm_size, area_size,
    barrier_ref, tie_offset, tie_gain, slack_hbm, hess_hbm, grad_hbm, guess_hbm, tile_hbm, ramp_ref, coup_ref,
    sens_hbm, load_hbm, owner_ref,
    step_ref, resid_ref,
    raw, guess_ref, right_ref, diag_buf, tile_buf, tile_high, tile_low,
    sens_own, load_own, load_stack, sens_out, load_out, sens_got, load_got, sens_high, sens_low, weight_ref,
    tie_buf, field, acc, halo, hour_stage, hour_halo, coup_halo, red_stage, red_slots,
    load_sem, halo_send, halo_recv, hour_send, hour_recv, coup_send, coup_recv, red_send, red_recv,
    sens_send, sens_recv, load_send, load_recv, pass_send, pass_recv, relay_send,
):
    span, padded, width = guess_ref.shape
    parts = width // 128
    plane = Y_SIZE * CORES
    zeds = area_size // plane
    per_device = span * CAPACITY
    me_t = lax.axis_index("tm")
    me_a = lax.axis_index("area")
    zed = lax.div(me_a, plane)
    place = lax.rem(me_a, plane)
    wye = lax.div(place, CORES)
    core = lax.rem(place, CORES)
    count_one = tm_size * Y_SIZE
    count_two = area_size // Y_SIZE
    mine = (me_t * Y_SIZE + wye, zed * CORES + core)
    counts = (count_one, count_two)

    def partner(stage, index):
        if stage == 0:
            t = lax.div(index, Y_SIZE)
            y = lax.rem(index, Y_SIZE)
            return (t, zed * plane + y * CORES + core)
        z = lax.div(index, CORES)
        c = lax.rem(index, CORES)
        return (me_t, z * plane + wye * CORES + c)

    above = (me_t, lax.rem(me_a + 1, area_size))
    below = (me_t, lax.rem(me_a + area_size - 1, area_size))
    later = (lax.rem(me_t + 1, tm_size), me_a)
    earlier = (lax.rem(me_t + tm_size - 1, tm_size), me_a)

    quarter = pl.multiple_of(me_t * 128, 128)
    sens_load = pltpu.make_async_copy(sens_hbm.at[:, pl.ds(quarter, 128)], sens_own, load_sem.at[0])
    load_load = pltpu.make_async_copy(load_hbm, load_own, load_sem.at[1])
    raw_loads = [
        pltpu.make_async_copy(source, raw.at[k], load_sem.at[2 + k])
        for k, source in enumerate((guess_hbm, slack_hbm, hess_hbm, grad_hbm))
    ]
    tile_load = pltpu.make_async_copy(tile_hbm, tile_buf, load_sem.at[6])
    for copy in [sens_load, load_load] + raw_loads + [tile_load]:
        copy.start()

    barrier = pltpu.get_barrier_semaphore()
    greeted = 0
    for d in range(1, area_size):
        other = (me_t, lax.rem(me_a + d, area_size))
        pl.semaphore_signal(barrier, inc=1, device_id=other, device_id_type=MESH)
        greeted += 1
    for dt in range(1, tm_size):
        for y in range(Y_SIZE):
            other = (lax.rem(me_t + dt, tm_size), zed * plane + y * CORES + core)
            pl.semaphore_signal(barrier, inc=1, device_id=other, device_id_type=MESH)
            greeted += 1

    rows_held = sens_own.shape[0]
    areas = area_size * span
    owner = jnp.broadcast_to(owner_ref[...], (areas, rows_held))
    marks = jnp.where(owner == lax.broadcasted_iota(jnp.int32, owner.shape, 0), 1.0, 0.0)
    earlier_row = lax.broadcasted_iota(jnp.int32, (rows_held, rows_held), 0)
    this_row = lax.broadcasted_iota(jnp.int32, (rows_held, rows_held), 1)
    order = jnp.where(earlier_row < this_row, 1.0, 0.0).astype(BF16)
    marks_low = marks.astype(BF16)
    ahead = jnp.dot(marks_low, order, preferred_element_type=F32)
    rank = jnp.sum(ahead * marks, axis=0, keepdims=True)
    slot = owner_ref[...] * CAPACITY + rank.astype(jnp.int32)
    slots = areas * CAPACITY
    wide = jnp.broadcast_to(slot, (slots, rows_held))
    pick = jnp.where(wide == lax.broadcasted_iota(jnp.int32, wide.shape, 0), 1.0, 0.0).astype(BF16)

    def thirds(x):
        high = x.astype(BF16)
        rest = x - high.astype(F32)
        middle = rest.astype(BF16)
        return high, middle, (rest - middle.astype(F32)).astype(BF16)

    sens_load.wait()
    moved = [jnp.dot(pick, part, preferred_element_type=F32) for part in thirds(sens_own[...])]
    sens_out[...] = (moved[0] + moved[1] + moved[2]).reshape(area_size, per_device, 128)
    load_load.wait()
    loads = load_own[...]
    load_stack[...] = jnp.zeros_like(load_stack)
    load_stack[0:hours, :] = jnp.where(rank < 0.5, loads, 0.0)
    load_stack[64 : 64 + hours, :] = jnp.where(rank > 0.5, loads, 0.0)
    moved = [
        lax.dot_general(marks_low, part, NT, preferred_element_type=F32) for part in thirds(load_stack[...])
    ]
    load_out[...] = (moved[0] + moved[1] + moved[2]).reshape(area_size, span, 128)

    pl.semaphore_wait(barrier, greeted)

    def remote(source, target, send, recv, device):
        return pltpu.make_async_remote_copy(
            src_ref=source, dst_ref=target, send_sem=send, recv_sem=recv,
            device_id=device, device_id_type=MESH,
        )

    steps = [0]
    for d in range(1, (zeds + 1) // 2):
        steps += [d, -d]
    if zeds % 2 == 0:
        steps += [zeds // 2]
    steps = [d % zeds for d in steps]
    own_rows = pl.ds(pl.multiple_of(me_a * per_device, per_device), per_device)
    block_copies, load_copies = {}, {}
    for dz in steps:
        for e in range(plane):
            to = lax.rem(zed + dz, zeds) * plane + lax.rem(place + e, plane)
            key = ((zeds - dz) % zeds) * plane + (plane - e) % plane
            if dz == 0 and e == 0:
                block = pltpu.make_async_copy(sens_out.at[me_a], sens_got.at[me_t, own_rows], sens_recv.at[key])
                load = pltpu.make_async_copy(load_out.at[me_a], load_got.at[me_a], load_recv.at[key])
            else:
                block = remote(
                    sens_out.at[to], sens_got.at[me_t, own_rows], sens_send.at[key], sens_recv.at[key], (me_t, to)
                )
                load = remote(load_out.at[to], load_got.at[me_a], load_send.at[key], load_recv.at[key], (me_t, to))
            block.start()
            load.start()
            block_copies[key] = block
            load_copies[key] = load

    coup_copies = [
        remote(coup_ref, coup_halo.at[0], coup_send.at[0], coup_recv.at[0], above),
        remote(coup_ref, coup_halo.at[1], coup_send.at[1], coup_recv.at[1], below),
    ]
    for copy in coup_copies:
        copy.start()

    def piece(i, j):
        return pl.ds(j * span + i, hours, stride=span * parts)

    def columns(j):
        return slice(j * 128, (j + 1) * 128)

    raw_loads[0].wait()
    for i in range(span):
        guess_ref[i, padded - 8 : padded, :] = jnp.zeros((8, width), F32)
        for j in range(parts):
            guess_ref[i, 0:hours, columns(j)] = raw[0, piece(i, j), :]

    def stage_hours(phase, source):
        for i in range(span):
            hour_stage[phase, 0, i : i + 1, :] = source[i, 0:1, :]
            hour_stage[phase, 1, i : i + 1, :] = source[i, hours - 1 : hours, :]

    stage_hours(0, guess_ref)

    def field_copies(phase, source, i):
        return [
            remote(source.at[i], halo.at[phase, 0, i], halo_send.at[phase, 0, i], halo_recv.at[phase, 0, i], above),
            remote(source.at[i], halo.at[phase, 1, i], halo_send.at[phase, 1, i], halo_recv.at[phase, 1, i], below),
        ]

    def hour_copies(phase):
        return [
            remote(hour_stage.at[phase, 1], hour_halo.at[phase, 0], hour_send.at[phase, 0], hour_recv.at[phase, 0], later),
            remote(hour_stage.at[phase, 0], hour_halo.at[phase, 1], hour_send.at[phase, 1], hour_recv.at[phase, 1], earlier),
        ]

    flying = [[], [], []]
    for i in range(span):
        flying[0] += field_copies(0, guess_ref, i)
    flying[0] += hour_copies(0)
    for copy in flying[0]:
        copy.start()

    for copy in raw_loads[1:]:
        copy.wait()
    scale = barrier_ref[0]
    for i in range(span):
        diag_buf[i, padded - 8 : padded, :] = jnp.zeros((8, width), F32)
        right_ref[i, padded - 8 : padded, :] = jnp.zeros((8, width), F32)
        for j in range(parts):
            slack = raw[1, piece(i, j), :]
            diag_buf[i, 0:hours, columns(j)] = raw[2, piece(i, j), :] + scale / (slack * slack)
            right_ref[i, 0:hours, columns(j)] = scale / slack - raw[3, piece(i, j), :]

    tile_load.wait()
    for i in range(span):
        high, low = split(tile_buf[i])
        tile_high[i] = high
        tile_low[i] = low

    first = me_a * span

    def gains_of(start, valid):
        table = []
        for r in range(span):
            area = start + r
            row = []
            for o in range(1, TIES + 1):
                total = jnp.float32(0.0)
                for k in range(TIES):
                    total = total + jnp.where(tie_offset[k, area] == o, tie_gain[k, area], 0.0)
                inside = jnp.logical_and(valid, area + o < areas)
                row.append(jnp.where(inside, total, 0.0))
            table.append(row)
        return table

    lower_start = lax.rem(me_a + area_size - 1, area_size) * span
    window = gains_of(lower_start, me_a > 0) + gains_of(first, me_a >= 0)

    for copy in coup_copies:
        copy.wait()
    coupling = [coup_halo[0, i : i + 1, :] for i in range(span)]
    coupling += [coup_ref[i : i + 1, :] for i in range(span)]
    coupling += [coup_halo[1, i : i + 1, :] for i in range(span)]
    offsets = [o for o in range(-TIES, TIES + 1) if o != 0]
    for i in range(span):
        total = 2.0 * ramp_ref[i : i + 1, :]
        for k, o in enumerate(offsets):
            gain = window[span + i][o - 1] if o > 0 else window[span + i + o][-o - 1]
            row = coupling[span + i] * coupling[span + i + o] * gain
            tie_buf[i, k : k + 1, :] = row
            total = total + row
        diag_buf[i] = diag_buf[i] + total

    def tile_part(value, i):
        high, low = split(value)
        stacked = jnp.concatenate([high, low], axis=0)
        return product(stacked, high, tile_high[i], tile_low[i], NN)

    def security_part(value, i):
        high, low = split(value)
        stacked = jnp.concatenate([high, low], axis=0)
        flow = product(stacked, high, sens_high[i], sens_low[i], NT) * weight_ref[i]
        flow_high, flow_low = split(flow)
        flow_stacked = jnp.concatenate([flow_high, flow_low], axis=0)
        return product(flow_stacked, flow_high, sens_high[i], sens_low[i], NN)

    def local_part(value, i):
        return tile_part(value, i) + security_part(value, i)

    for i in range(span):
        acc[i] = tile_part(guess_ref[i], i)

    group = plane * per_device
    passes, relays = [], []

    def group_rows(k):
        z = lax.rem(zed + steps[k], zeds)
        return pl.ds(pl.multiple_of(z * group, group), group)

    def relay(k):
        forward = k % 2 == 0
        passes[k][0 if forward else 1].wait_recv()
        origin = lax.rem(me_t + (tm_size - 1 if forward else 1), tm_size)
        there = sens_got.at[origin, group_rows(k)]
        copy = remote(there, there, relay_send.at[k], pass_recv.at[k, 2], later if forward else earlier)
        copy.start()
        relays.append(copy)

    for k in range(zeds):
        for e in range(plane):
            key = steps[k] * plane + e
            if key == 0:
                block_copies[key].wait()
            else:
                block_copies[key].wait_recv()
        here = sens_got.at[me_t, group_rows(k)]
        pair = [
            remote(here, here, pass_send.at[k, 0], pass_recv.at[k, 0], later),
            remote(here, here, pass_send.at[k, 1], pass_recv.at[k, 1], earlier),
        ]
        for copy in pair:
            copy.start()
        passes.append(pair)
        if k >= 1:
            relay(k - 1)
    relay(zeds - 1)
    for key, copy in load_copies.items():
        if key == 0:
            copy.wait()
        else:
            copy.wait_recv()
    for i in range(span):
        seen = load_got[:, i, :].T
        weight_ref[i] = jnp.concatenate([seen[0:padded], seen[64 : 64 + padded]], axis=1)
    for k in range(zeds):
        passes[k][1 if k % 2 == 0 else 0].wait_recv()
        relays[k].wait_recv()
    for i in range(span):
        for q in range(parts):
            for c in range(CAPACITY):
                high, low = split(sens_got[q, pl.ds(i * CAPACITY + c, area_size, stride=per_device), :])
                sens_high[i, c * area_size : (c + 1) * area_size, columns(q)] = high
                sens_low[i, c * area_size : (c + 1) * area_size, columns(q)] = low

    rows = lax.broadcasted_iota(jnp.int32, (padded, width), 0)
    first_hours = me_t == 0
    last_hours = me_t == tm_size - 1

    def finish(phase, source, i):
        value = source[i]
        before = hour_halo[phase, 0, i : i + 1, :]
        before = jnp.where(first_hours, jnp.zeros_like(before), before)
        after = hour_halo[phase, 1, i : i + 1, :]
        after = jnp.where(last_hours, jnp.zeros_like(after), after)
        up = jnp.where(rows == hours - 1, after, pltpu.roll(value, padded - 1, 0))
        down = jnp.where(rows == 0, before, pltpu.roll(value, 1, 0))
        out = acc[i] + diag_buf[i] * value - ramp_ref[i : i + 1, :] * (up + down)
        for k, o in enumerate(offsets):
            j = i + o
            if j < 0:
                near = halo[phase, 0, span + j]
            elif j < span:
                near = source[j]
            else:
                near = halo[phase, 1, j - span]
            out = out - tie_buf[i, k : k + 1, :] * near
        return jnp.where(rows < hours, out, jnp.zeros_like(out))

    def start_stage(which, stage):
        copies = []
        for d in range(1, counts[stage]):
            to = lax.rem(mine[stage] + d, counts[stage])
            copy = remote(
                red_stage.at[which, stage], red_slots.at[which, stage, mine[stage]],
                red_send.at[which, stage, d], red_recv.at[which, stage, d], partner(stage, to),
            )
            copy.start()
            copies.append(copy)
        return copies

    def end_stage(which, stage, copies):
        for copy in copies:
            copy.wait()
        total = jnp.zeros((8, 128), F32)
        for s in range(counts[stage]):
            total = total + red_slots[which, stage, s]
        return total

    def begin(which, stage, tile):
        red_stage[which, stage] = tile
        red_slots[which, stage, mine[stage]] = tile
        return start_stage(which, stage)

    def pack(values):
        filled = jnp.zeros((8 - len(values), 128), F32)
        return jnp.concatenate(values + [filled], axis=0)

    def send_phase(phase, source):
        copies = []
        for i in range(span):
            copies += field_copies(phase, source, i)
        stage_hours(phase, source)
        copies += hour_copies(phase)
        for copy in copies:
            copy.start()
        flying[phase] = copies

    for i in range(span):
        acc[i] = acc[i] + security_part(guess_ref[i], i)
    for copy in flying[0]:
        copy.wait()
    sum_rr = jnp.zeros((1, 128), F32)
    for i in range(span):
        value = right_ref[i] - finish(0, guess_ref, i)
        field[0, i] = value
        sum_rr = sum_rr + lane_sum(value * value)
    send_phase(1, field.at[0])
    for i in range(span):
        acc[i] = local_part(field[0, i], i)
    for copy in flying[1]:
        copy.wait()
    sum_rv = jnp.zeros((1, 128), F32)
    for i in range(span):
        value = finish(1, field.at[0], i)
        field[1, i] = value
        sum_rv = sum_rv + lane_sum(value * field[0, i])
    send_phase(2, field.at[1])
    copies = begin(0, 0, pack([sum_rr, sum_rv]))
    half = span // 2
    for i in range(half):
        acc[i] = local_part(field[1, i], i)
    total = end_stage(0, 0, copies)
    copies = begin(0, 1, total)
    for i in range(half, span):
        acc[i] = local_part(field[1, i], i)
    for copy in flying[2]:
        copy.wait()
    for i in range(span):
        field[2, i] = finish(2, field.at[1], i)
    total = jnp.sum(end_stage(0, 1, copies), axis=1, keepdims=True)
    rr_zero, rv_zero = total[0:1], total[1:2]
    alpha_zero = rr_zero / rv_zero

    sums = [jnp.zeros((1, 128), F32) for _ in range(4)]
    for i in range(span):
        zero, one, two = field[0, i], field[1, i], field[2, i]
        resid = zero - alpha_zero * one
        image = one - alpha_zero * two
        field[2, i] = image
        acc[i] = resid
        sums[0] = sums[0] + lane_sum(resid * resid)
        sums[1] = sums[1] + lane_sum(resid * image)
        sums[2] = sums[2] + lane_sum(resid * one)
        sums[3] = sums[3] + lane_sum(zero * image)
    copies = begin(1, 0, pack(sums))
    total = end_stage(1, 0, copies)
    copies = begin(1, 1, total)
    total = jnp.sum(end_stage(1, 1, copies), axis=1, keepdims=True)
    beta = total[0:1] / rr_zero
    bend = total[1:2] + beta * (total[2:3] + total[3:4]) + beta * beta * rv_zero
    alpha_one = total[0:1] / bend
    for i in range(span):
        resid = acc[i]
        zero = field[0, i]
        step = guess_ref[i] + alpha_zero * zero + alpha_one * (resid + beta * zero)
        final = resid - alpha_one * (field[2, i] + beta * field[1, i])
        for j in range(parts):
            step_ref[piece(i, j), :] = step[0:hours, columns(j)]
            resid_ref[piece(i, j), :] = final[0:hours, columns(j)]
    for key in range(1, area_size):
        block_copies[key].wait_send()
        load_copies[key].wait_send()
    for k in range(zeds):
        for copy in passes[k]:
            copy.wait_send()
        relays[k].wait_send()


def body(
    gradient, barrier, slack, hess_diag, tile, ramp_weight, bus_coupling, tie_offset, tie_admittance,
    con_sens, con_weight, con_owner, step_guess,
):
    hours, span, width = gradient.shape
    tm_size, area_size = lax.axis_size("tm"), lax.axis_size("area")
    rows_held = con_sens.shape[0]
    parts = width // 128
    padded = -(-hours // 8) * 8
    per_device = span * CAPACITY
    zeds = area_size // (Y_SIZE * CORES)
    most = max(tm_size * Y_SIZE, area_size // Y_SIZE)
    own_slots = area_size * CAPACITY

    def rows_of(x):
        return jnp.transpose(x.reshape(hours, span, parts, 128), (0, 2, 1, 3)).reshape(hours * parts * span, 128)

    def field_of(x):
        return jnp.transpose(x.reshape(hours, parts, span, 128), (0, 2, 1, 3)).reshape(hours, span, width)

    vmem = pl.BlockSpec(memory_space=pltpu.VMEM)
    smem = pl.BlockSpec(memory_space=pltpu.SMEM)
    anywhere = pl.BlockSpec(memory_space=pl.ANY)
    dma = pltpu.SemaphoreType.DMA
    flat = jax.ShapeDtypeStruct((hours * parts * span, 128), F32)
    block = (span, padded, width)
    step, residual = pl.pallas_call(
        functools.partial(kernel, hours, tm_size, area_size),
        out_shape=(flat, flat),
        in_specs=[smem] * 3 + [anywhere] * 5 + [vmem] * 2 + [anywhere] * 2 + [vmem],
        out_specs=(vmem, vmem),
        scratch_shapes=[
            pltpu.VMEM((4,) + flat.shape, F32),
            pltpu.VMEM(block, F32), pltpu.VMEM(block, F32), pltpu.VMEM(block, F32),
            pltpu.VMEM(tile.shape, F32), pltpu.VMEM(tile.shape, BF16), pltpu.VMEM(tile.shape, BF16),
            pltpu.VMEM((rows_held, 128), F32), pltpu.VMEM((hours, rows_held), F32), pltpu.VMEM((128, rows_held), F32),
            pltpu.VMEM((area_size, per_device, 128), F32), pltpu.VMEM((area_size, span, 128), F32),
            pltpu.VMEM((parts, area_size * per_device, 128), F32), pltpu.VMEM((area_size, span, 128), F32),
            pltpu.VMEM((span, own_slots, width), BF16), pltpu.VMEM((span, own_slots, width), BF16),
            pltpu.VMEM((span, padded, own_slots), F32),
            pltpu.VMEM((span, 2 * TIES, width), F32),
            pltpu.VMEM((3,) + block, F32),
            pltpu.VMEM(block, F32),
            pltpu.VMEM((3, 2) + block, F32),
            pltpu.VMEM((3, 2, span, width), F32), pltpu.VMEM((3, 2, span, width), F32), pltpu.VMEM((2, span, width), F32),
            pltpu.VMEM((2, 2, 8, 128), F32), pltpu.VMEM((2, 2, most, 8, 128), F32),
            dma((7,)), dma((3, 2, span)), dma((3, 2, span)), dma((3, 2)), dma((3, 2)), dma((2,)), dma((2,)),
            dma((2, 2, most)), dma((2, 2, most)),
            dma((area_size,)), dma((area_size,)), dma((area_size,)), dma((area_size,)),
            dma((zeds, 2)), dma((zeds, 3)), dma((zeds,)),
        ],
        compiler_params=pltpu.CompilerParams(collective_id=0, has_side_effects=True, vmem_limit_bytes=60 * 1024 * 1024),
    )(
        barrier, tie_offset.T, tie_admittance.T, rows_of(slack), rows_of(hess_diag), rows_of(gradient),
        rows_of(step_guess), tile, ramp_weight, bus_coupling, con_sens, con_weight.T, con_owner.T,
    )
    return field_of(step), field_of(residual)


def solution(mesh):
    placed = (
        P("tm", "area", None), P(), P("tm", "area", None), P("tm", "area", None), P("area", None, None),
        P("area", None), P("area", None), P(), P(), P("area", None), P("area", "tm"), P("area", None),
        P("tm", "area", None),
    )
    return jax.shard_map(
        body, mesh=mesh, in_specs=placed,
        out_specs=(P("tm", "area", None), P("tm", "area", None)), check_vma=False,
    )
```

time: 118 us -> 82.4 us (0.70)
  Pallas kernels: 47.9 us -> 77.4 us
  waiting for transfers between devices: 28.9 us -> 0 us
  starting transfers between devices: 17.6 us -> 0 us
  local copies, waits for them, and re-layouts: 18.1 us -> 3.46 us
  other arithmetic: 3.15 us -> 0 us
    pallas_call x1, Pallas kernels: 47.9 us -> 77.4 us  [body(): pl.pallas_call(functools.partial(kernel, hours, tm_size, area_size), out_...]
    all_to_all x2 -> x0, waiting for transfers between devices: 28.9 us -> none  [the longest x1 21.2 us: body(): lax.all_to_all(send_sens, 'area', split_axis=0, concat_axis=0, tiled=True)]
    all_to_all x2 -> x0, starting transfers between devices: 17.6 us -> none  [the longest x1 13.1 us: body(): lax.all_to_all(send_weight, 'area', split_axis=0, concat_axis=0, tiled=True)]
    scatter x2 -> x0, local copies, waits for them, and re-layouts: 4.14 us -> none  [the longest x1 2.93 us: body(): jnp.zeros((area_total * capacity, var_width), F32).at[slot_index]]
    pad x4 -> x0, local copies, waits for them, and re-layouts: 3 us -> none  [the longest x3 2.35 us: by_area(): return jnp.pad(jnp.transpose(x, (1, 0, 2)), fill)]
    transpose x3 -> x0, local copies, waits for them, and re-layouts: 2.19 us -> none  [the longest x1 1.19 us: body(): jnp.transpose(residual[:, :hour_count], (1, 0, 2))]
    reshape x2 -> x0, local copies, waits for them, and re-layouts: 1.84 us -> none  [the longest x1 1.71 us: body(): owned_sens = jnp.transpose(got_sens.reshape(groups, span_areas, capacity,...]
    all_to_all x3 -> x0, local copies, waits for them, and re-layouts: 1.3 us -> none  [the longest x2 0.69 us: body(): lax.all_to_all(send_weight, 'area', split_axis=0, concat_axis=0, tiled=True)]
  transfers between devices with their start and end apart: 2 -> 0, of which waited for: 2 -> 0; matrix products, arithmetic and copies ran while one was open for 8% -> 0% of each run, Pallas kernels for 0% -> 0%
where the time goes in v1:
time: 82.4 us; the launch traced here: 82.2 us
  Pallas kernels  77.4 us (94%)
  local copies, waits for them, and re-layouts  3.46 us (4%)
  between operations  1.29 us (2%)
    pallas_call x1, Pallas kernels, body(): pl.pallas_call(functools.partial(kernel, hours, tm_size, area_size), out_...  77.4 us
    unnamed x2, local copies, waits for them, and re-layouts  3.46 us

profile of v1, /device:TPU:1, one launch (start us, length us, event | category | flops | bytes accessed | tf_op | source)
XLA Modules:
  0.0 82.2 jit_solution(1751366145670945297)
XLA Ops:
  1.3 77.4 %shard_map.140 = (f32[672,128]{1,0:T(8,128)}, f32[672,128]{1,0:T(8,128)}) custom-call(f32[1]{0:T(128)S(6)} %copy.23.barrier_ref, s32[4,256]{1,0:T(4,128)} %bitcast.41, f32[4,256]{1,0:T(4,128)} %bitcast.42, f32[672,128]{1,0:T(8,128)} %bitcast.36, f32[672,128]{1,0:T(8,128)} %bitcast.37, f32[672,128]{1,0:T(8,128)} %bitcast.38, f32[672,128]{1,0:T(8,128)} %bitcast.39, ...), custom_call_target="tpu_custom_call" | custom-call | tf_op jit(solution)/shard_map/pallas_call | solution.py:502
  78.7 1.7 %copy.24 = f32[42,4,512]{2,1,0:T(4,128)} copy(f32[42,4,512]{2,1,0:T(4,128)} %bitcast.35) | data formatting | bytes 688128
  80.4 1.7 %copy.25 = f32[42,4,512]{2,1,0:T(4,128)} copy(f32[42,4,512]{2,1,0:T(4,128)} %bitcast.34) | data formatting | bytes 688128

commit v2 on v1

--- a/solution.py
+++ b/solution.py
@@ -168,10 +168,11 @@
                 )
                 load = remote(load_out.at[to], load_got.at[me_a], load_send.at[key], load_recv.at[key], (me_t, to))
             block.start()
-            load.start()
             block_copies[key] = block
             load_copies[key] = load
 
+    for copy in load_copies.values():
+        copy.start()
     coup_copies = [
         remote(coup_ref, coup_halo.at[0], coup_send.at[0], coup_recv.at[0], above),
         remote(coup_ref, coup_halo.at[1], coup_send.at[1], coup_recv.at[1], below),
@@ -196,13 +197,13 @@
             hour_stage[phase, 0, i : i + 1, :] = source[i, 0:1, :]
             hour_stage[phase, 1, i : i + 1, :] = source[i, hours - 1 : hours, :]
 
-    stage_hours(0, guess_ref)
-
-    def field_copies(phase, source, i):
-        return [
-            remote(source.at[i], halo.at[phase, 0, i], halo_send.at[phase, 0, i], halo_recv.at[phase, 0, i], above),
-            remote(source.at[i], halo.at[phase, 1, i], halo_send.at[phase, 1, i], halo_recv.at[phase, 1, i], below),
-        ]
+    def send_area(phase, source, side, i):
+        copy = remote(
+            source.at[i], halo.at[phase, side, i], halo_send.at[phase, side, i], halo_recv.at[phase, side, i],
+            below if side else above,
+        )
+        copy.start()
+        flying[phase][side, i] = copy
 
     def hour_copies(phase):
         return [
@@ -210,12 +211,19 @@
             remote(hour_stage.at[phase, 0], hour_halo.at[phase, 1], hour_send.at[phase, 1], hour_recv.at[phase, 1], earlier),
         ]
 
-    flying = [[], [], []]
-    for i in range(span):
-        flying[0] += field_copies(0, guess_ref, i)
-    flying[0] += hour_copies(0)
-    for copy in flying[0]:
-        copy.start()
+    def send_hours(phase, source):
+        stage_hours(phase, source)
+        for side, copy in enumerate(hour_copies(phase)):
+            copy.start()
+            flying[phase]["hours", side] = copy
+
+    ready = (1, 2, 0, 3)
+    sends = {1: [(1, 1)], 2: [(0, 2), (0, 1), (1, 2)], 0: [(1, 0)], 3: [(0, 3), (0, 0), (1, 3)]}
+    flying = [{}, {}, {}]
+    send_hours(0, guess_ref)
+    for i in ready:
+        for side, j in sends[i]:
+            send_area(0, guess_ref, side, j)
 
     for copy in raw_loads[1:]:
         copy.wait()
@@ -284,8 +292,53 @@
     def local_part(value, i):
         return tile_part(value, i) + security_part(value, i)
 
+    rows = lax.broadcasted_iota(jnp.int32, (padded, width), 0)
+    first_hours = me_t == 0
+    last_hours = me_t == tm_size - 1
+
+    def near_part(source, i):
+        value = source[i]
+        beside = pltpu.roll(value, padded - 1, 0) + pltpu.roll(value, 1, 0)
+        beside = jnp.where(rows < hours, beside, jnp.zeros_like(beside))
+        out = acc[i] + diag_buf[i] * value - ramp_ref[i : i + 1, :] * beside
+        for k, o in enumerate(offsets):
+            if 0 <= i + o < span:
+                out = out - tie_buf[i, k : k + 1, :] * source[i + o]
+        acc[i] = out
+
+    def hour_part(phase):
+        for side in range(2):
+            flying[phase]["hours", side].wait_recv()
+        for i in range(span):
+            ramp = ramp_ref[i : i + 1, :]
+            before = ramp * hour_halo[phase, 0, i : i + 1, :]
+            after = ramp * hour_halo[phase, 1, i : i + 1, :]
+            acc[i, 0:1, :] = acc[i, 0:1, :] - jnp.where(first_hours, jnp.zeros_like(before), before)
+            acc[i, hours - 1 : hours, :] = acc[i, hours - 1 : hours, :] - jnp.where(
+                last_hours, jnp.zeros_like(after), after
+            )
+
+    def halo_part(phase, pieces):
+        for piece_key in pieces:
+            flying[phase][piece_key].wait_recv()
+        for i in range(span):
+            terms = []
+            for side, j in pieces:
+                o = span + j - i if side else j - span - i
+                if abs(o) <= TIES:
+                    k = offsets.index(o)
+                    terms.append(tie_buf[i, k : k + 1, :] * halo[phase, side, j])
+            if terms:
+                acc[i] = acc[i] - functools.reduce(lambda x, y: x + y, terms)
+
+    pieces_one = [(0, 2), (1, 1)]
+    pieces_two = [(0, 1), (1, 2)]
+    pieces_three = [(0, 3), (1, 0)]
+    pieces_four = [(0, 0), (1, 3)]
+
     for i in range(span):
         acc[i] = tile_part(guess_ref[i], i)
+        near_part(guess_ref, i)
 
     group = plane * per_device
     passes, relays = [], []
@@ -329,39 +382,25 @@
     for i in range(span):
         seen = load_got[:, i, :].T
         weight_ref[i] = jnp.concatenate([seen[0:padded], seen[64 : 64 + padded]], axis=1)
+    def place_columns(origin):
+        where = pl.ds(pl.multiple_of(origin * 128, 128), 128)
+        for i in range(span):
+            for c in range(CAPACITY):
+                high, low = split(sens_got[origin, pl.ds(i * CAPACITY + c, area_size, stride=per_device), :])
+                sens_high[i, c * area_size : (c + 1) * area_size, where] = high
+                sens_low[i, c * area_size : (c + 1) * area_size, where] = low
+
+    place_columns(me_t)
+    hour_part(0)
+    for pieces in (pieces_one, pieces_two, pieces_three, pieces_four):
+        halo_part(0, pieces)
     for k in range(zeds):
         passes[k][1 if k % 2 == 0 else 0].wait_recv()
+    place_columns(lax.rem(me_t + tm_size - 1, tm_size))
+    place_columns(lax.rem(me_t + 1, tm_size))
+    for k in range(zeds):
         relays[k].wait_recv()
-    for i in range(span):
-        for q in range(parts):
-            for c in range(CAPACITY):
-                high, low = split(sens_got[q, pl.ds(i * CAPACITY + c, area_size, stride=per_device), :])
-                sens_high[i, c * area_size : (c + 1) * area_size, columns(q)] = high
-                sens_low[i, c * area_size : (c + 1) * area_size, columns(q)] = low
-
-    rows = lax.broadcasted_iota(jnp.int32, (padded, width), 0)
-    first_hours = me_t == 0
-    last_hours = me_t == tm_size - 1
-
-    def finish(phase, source, i):
-        value = source[i]
-        before = hour_halo[phase, 0, i : i + 1, :]
-        before = jnp.where(first_hours, jnp.zeros_like(before), before)
-        after = hour_halo[phase, 1, i : i + 1, :]
-        after = jnp.where(last_hours, jnp.zeros_like(after), after)
-        up = jnp.where(rows == hours - 1, after, pltpu.roll(value, padded - 1, 0))
-        down = jnp.where(rows == 0, before, pltpu.roll(value, 1, 0))
-        out = acc[i] + diag_buf[i] * value - ramp_ref[i : i + 1, :] * (up + down)
-        for k, o in enumerate(offsets):
-            j = i + o
-            if j < 0:
-                near = halo[phase, 0, span + j]
-            elif j < span:
-                near = source[j]
-            else:
-                near = halo[phase, 1, j - span]
-            out = out - tie_buf[i, k : k + 1, :] * near
-        return jnp.where(rows < hours, out, jnp.zeros_like(out))
+    place_columns(lax.rem(me_t + 2, tm_size))
 
     def start_stage(which, stage):
         copies = []
@@ -378,7 +417,7 @@
     def end_stage(which, stage, copies):
         for copy in copies:
             copy.wait()
-        total = jnp.zeros((8, 128), F32)
+        total = jnp.zeros((1, 128), F32)
         for s in range(counts[stage]):
             total = total + red_slots[which, stage, s]
         return total
@@ -388,59 +427,73 @@
         red_slots[which, stage, mine[stage]] = tile
         return start_stage(which, stage)
 
+    lanes = lax.broadcasted_iota(jnp.int32, (1, 128), 1)
+
     def pack(values):
-        filled = jnp.zeros((8 - len(values), 128), F32)
-        return jnp.concatenate(values + [filled], axis=0)
-
-    def send_phase(phase, source):
-        copies = []
-        for i in range(span):
-            copies += field_copies(phase, source, i)
-        stage_hours(phase, source)
-        copies += hour_copies(phase)
-        for copy in copies:
-            copy.start()
-        flying[phase] = copies
-
-    for i in range(span):
-        acc[i] = acc[i] + security_part(guess_ref[i], i)
-    for copy in flying[0]:
-        copy.wait()
+        total = jnp.zeros((1, 128), F32)
+        for k, value in enumerate(values):
+            total = jnp.where(lanes == k, jnp.sum(value, axis=1, keepdims=True), total)
+        return total
+
+    def take(total, k):
+        return jnp.sum(jnp.where(lanes == k, total, jnp.zeros_like(total)), axis=1, keepdims=True)
+
     sum_rr = jnp.zeros((1, 128), F32)
-    for i in range(span):
-        value = right_ref[i] - finish(0, guess_ref, i)
+    for i in ready:
+        value = right_ref[i] - (acc[i] + security_part(guess_ref[i], i))
         field[0, i] = value
+        for side, j in sends[i]:
+            send_area(1, field.at[0], side, j)
         sum_rr = sum_rr + lane_sum(value * value)
-    send_phase(1, field.at[0])
-    for i in range(span):
+    send_hours(1, field.at[0])
+    for i in ready:
         acc[i] = local_part(field[0, i], i)
-    for copy in flying[1]:
-        copy.wait()
+        near_part(field.at[0], i)
     sum_rv = jnp.zeros((1, 128), F32)
-    for i in range(span):
-        value = finish(1, field.at[0], i)
-        field[1, i] = value
-        sum_rv = sum_rv + lane_sum(value * field[0, i])
-    send_phase(2, field.at[1])
+    halo_part(1, pieces_one)
+    halo_part(1, pieces_two)
+    hour_part(1)
+    halo_part(1, pieces_three)
+    for i in ready[:2]:
+        field[1, i] = acc[i]
+        for side, j in sends[i]:
+            send_area(2, field.at[1], side, j)
+    for i in ready[:2]:
+        sum_rv = sum_rv + lane_sum(field[1, i] * field[0, i])
+    acc[ready[0]] = local_part(field[1, ready[0]], ready[0])
+    for piece_key in pieces_four:
+        flying[1][piece_key].wait_recv()
+    for i, (side, j) in zip(ready[2:], pieces_four):
+        k = offsets.index(span + j - i if side else j - span - i)
+        field[1, i] = acc[i] - tie_buf[i, k : k + 1, :] * halo[1, side, j]
+        for side, j in sends[i]:
+            send_area(2, field.at[1], side, j)
+    send_hours(2, field.at[1])
+    for i in ready[2:]:
+        sum_rv = sum_rv + lane_sum(field[1, i] * field[0, i])
     copies = begin(0, 0, pack([sum_rr, sum_rv]))
-    half = span // 2
-    for i in range(half):
+    for i in ready[1:3]:
         acc[i] = local_part(field[1, i], i)
     total = end_stage(0, 0, copies)
     copies = begin(0, 1, total)
-    for i in range(half, span):
-        acc[i] = local_part(field[1, i], i)
-    for copy in flying[2]:
-        copy.wait()
-    for i in range(span):
-        field[2, i] = finish(2, field.at[1], i)
-    total = jnp.sum(end_stage(0, 1, copies), axis=1, keepdims=True)
-    rr_zero, rv_zero = total[0:1], total[1:2]
+    acc[ready[3]] = local_part(field[1, ready[3]], ready[3])
+    for i in ready:
+        near_part(field.at[1], i)
+    halo_part(2, pieces_one)
+    halo_part(2, pieces_two)
+    total = end_stage(0, 1, copies)
+    rr_zero, rv_zero = take(total, 0), take(total, 1)
     alpha_zero = rr_zero / rv_zero
+    for i in ready:
+        right_ref[i] = guess_ref[i] + alpha_zero * field[0, i]
+    hour_part(2)
+    halo_part(2, pieces_three)
 
     sums = [jnp.zeros((1, 128), F32) for _ in range(4)]
-    for i in range(span):
-        zero, one, two = field[0, i], field[1, i], field[2, i]
+    for i in ready:
+        if i == ready[2]:
+            halo_part(2, pieces_four)
+        zero, one, two = field[0, i], field[1, i], acc[i]
         resid = zero - alpha_zero * one
         image = one - alpha_zero * two
         field[2, i] = image
@@ -452,14 +505,15 @@
     copies = begin(1, 0, pack(sums))
     total = end_stage(1, 0, copies)
     copies = begin(1, 1, total)
-    total = jnp.sum(end_stage(1, 1, copies), axis=1, keepdims=True)
-    beta = total[0:1] / rr_zero
-    bend = total[1:2] + beta * (total[2:3] + total[3:4]) + beta * beta * rv_zero
-    alpha_one = total[0:1] / bend
+    total = end_stage(1, 1, copies)
+    rr_one = take(total, 0)
+    beta = rr_one / rr_zero
+    bend = take(total, 1) + beta * (take(total, 2) + take(total, 3)) + beta * beta * rv_zero
+    alpha_one = rr_one / bend
     for i in range(span):
         resid = acc[i]
         zero = field[0, i]
-        step = guess_ref[i] + alpha_zero * zero + alpha_one * (resid + beta * zero)
+        step = right_ref[i] + alpha_one * (resid + beta * zero)
         final = resid - alpha_one * (field[2, i] + beta * field[1, i])
         for j in range(parts):
             step_ref[piece(i, j), :] = step[0:hours, columns(j)]
@@ -471,6 +525,9 @@
         for copy in passes[k]:
             copy.wait_send()
         relays[k].wait_send()
+    for group_copies in flying:
+        for copy in group_copies.values():
+            copy.wait_send()
 
 
 def body(
@@ -518,7 +575,7 @@
             pltpu.VMEM(block, F32),
             pltpu.VMEM((3, 2) + block, F32),
             pltpu.VMEM((3, 2, span, width), F32), pltpu.VMEM((3, 2, span, width), F32), pltpu.VMEM((2, span, width), F32),
-            pltpu.VMEM((2, 2, 8, 128), F32), pltpu.VMEM((2, 2, most, 8, 128), F32),
+            pltpu.VMEM((2, 2, 1, 128), F32), pltpu.VMEM((2, 2, most, 1, 128), F32),
             dma((7,)), dma((3, 2, span)), dma((3, 2, span)), dma((3, 2)), dma((3, 2)), dma((2,)), dma((2,)),
             dma((2, 2, most)), dma((2, 2, most)),
             dma((area_size,)), dma((area_size,)), dma((area_size,)), dma((area_size,)),

time: 82.4 us -> 79.1 us (0.960)
  Pallas kernels: 77.4 us -> 74.1 us
    pallas_call x1, Pallas kernels: 77.4 us -> 74.1 us  [body(): pl.pallas_call(functools.partial(kernel, hours, tm_size, area_size), out_...]
where the time goes in v2:
time: 79.1 us; the launch traced here: 78.9 us
  Pallas kernels  74.1 us (94%)
  local copies, waits for them, and re-layouts  3.46 us (4%)
  between operations  1.29 us (2%)
    pallas_call x1, Pallas kernels, body(): pl.pallas_call(functools.partial(kernel, hours, tm_size, area_size), out_...  74.1 us
    unnamed x2, local copies, waits for them, and re-layouts  3.46 us

profile of v2, /device:TPU:1, one launch (start us, length us, event | category | flops | bytes accessed | tf_op | source)
XLA Modules:
  0.0 78.9 jit_solution(16305117347769229041)
XLA Ops:
  1.3 74.1 %shard_map.140 = (f32[672,128]{1,0:T(8,128)}, f32[672,128]{1,0:T(8,128)}) custom-call(f32[1]{0:T(128)S(6)} %copy.23.barrier_ref, s32[4,256]{1,0:T(4,128)} %bitcast.41, f32[4,256]{1,0:T(4,128)} %bitcast.42, f32[672,128]{1,0:T(8,128)} %bitcast.36, f32[672,128]{1,0:T(8,128)} %bitcast.37, f32[672,128]{1,0:T(8,128)} %bitcast.38, f32[672,128]{1,0:T(8,128)} %bitcast.39, ...), custom_call_target="tpu_custom_call" | custom-call | tf_op jit(solution)/shard_map/pallas_call | solution.py:559
  75.4 1.7 %copy.24 = f32[42,4,512]{2,1,0:T(4,128)} copy(f32[42,4,512]{2,1,0:T(4,128)} %bitcast.35) | data formatting | bytes 688128
  77.2 1.7 %copy.25 = f32[42,4,512]{2,1,0:T(4,128)} copy(f32[42,4,512]{2,1,0:T(4,128)} %bitcast.34) | data formatting | bytes 688128

commit v3 on v2

--- a/solution.py
+++ b/solution.py
@@ -139,6 +139,54 @@
     ]
     load_out[...] = (moved[0] + moved[1] + moved[2]).reshape(area_size, span, 128)
 
+    def piece(i, j):
+        return pl.ds(j * span + i, hours, stride=span * parts)
+
+    def columns(j):
+        return slice(j * 128, (j + 1) * 128)
+
+    raw_loads[0].wait()
+    for i in range(span):
+        guess_ref[i, padded - 8 : padded, :] = jnp.zeros((8, width), F32)
+        for j in range(parts):
+            guess_ref[i, 0:hours, columns(j)] = raw[0, piece(i, j), :]
+
+    for copy in raw_loads[1:]:
+        copy.wait()
+    scale = barrier_ref[0]
+    for i in range(span):
+        diag_buf[i, padded - 8 : padded, :] = jnp.zeros((8, width), F32)
+        right_ref[i, padded - 8 : padded, :] = jnp.zeros((8, width), F32)
+        for j in range(parts):
+            slack = raw[1, piece(i, j), :]
+            diag_buf[i, 0:hours, columns(j)] = raw[2, piece(i, j), :] + scale / (slack * slack)
+            right_ref[i, 0:hours, columns(j)] = scale / slack - raw[3, piece(i, j), :]
+
+    tile_load.wait()
+    for i in range(span):
+        high, low = split(tile_buf[i])
+        tile_high[i] = high
+        tile_low[i] = low
+
+    first = me_a * span
+
+    def gains_of(start, valid):
+        table = []
+        for r in range(span):
+            area = start + r
+            row = []
+            for o in range(1, TIES + 1):
+                total = jnp.float32(0.0)
+                for k in range(TIES):
+                    total = total + jnp.where(tie_offset[k, area] == o, tie_gain[k, area], 0.0)
+                inside = jnp.logical_and(valid, area + o < areas)
+                row.append(jnp.where(inside, total, 0.0))
+            table.append(row)
+        return table
+
+    lower_start = lax.rem(me_a + area_size - 1, area_size) * span
+    window = gains_of(lower_start, me_a > 0) + gains_of(first, me_a >= 0)
+
     pl.semaphore_wait(barrier, greeted)
 
     def remote(source, target, send, recv, device):
@@ -180,18 +228,6 @@
     for copy in coup_copies:
         copy.start()
 
-    def piece(i, j):
-        return pl.ds(j * span + i, hours, stride=span * parts)
-
-    def columns(j):
-        return slice(j * 128, (j + 1) * 128)
-
-    raw_loads[0].wait()
-    for i in range(span):
-        guess_ref[i, padded - 8 : padded, :] = jnp.zeros((8, width), F32)
-        for j in range(parts):
-            guess_ref[i, 0:hours, columns(j)] = raw[0, piece(i, j), :]
-
     def stage_hours(phase, source):
         for i in range(span):
             hour_stage[phase, 0, i : i + 1, :] = source[i, 0:1, :]
@@ -225,56 +261,7 @@
         for side, j in sends[i]:
             send_area(0, guess_ref, side, j)
 
-    for copy in raw_loads[1:]:
-        copy.wait()
-    scale = barrier_ref[0]
-    for i in range(span):
-        diag_buf[i, padded - 8 : padded, :] = jnp.zeros((8, width), F32)
-        right_ref[i, padded - 8 : padded, :] = jnp.zeros((8, width), F32)
-        for j in range(parts):
-            slack = raw[1, piece(i, j), :]
-            diag_buf[i, 0:hours, columns(j)] = raw[2, piece(i, j), :] + scale / (slack * slack)
-            right_ref[i, 0:hours, columns(j)] = scale / slack - raw[3, piece(i, j), :]
-
-    tile_load.wait()
-    for i in range(span):
-        high, low = split(tile_buf[i])
-        tile_high[i] = high
-        tile_low[i] = low
-
-    first = me_a * span
-
-    def gains_of(start, valid):
-        table = []
-        for r in range(span):
-            area = start + r
-            row = []
-            for o in range(1, TIES + 1):
-                total = jnp.float32(0.0)
-                for k in range(TIES):
-                    total = total + jnp.where(tie_offset[k, area] == o, tie_gain[k, area], 0.0)
-                inside = jnp.logical_and(valid, area + o < areas)
-                row.append(jnp.where(inside, total, 0.0))
-            table.append(row)
-        return table
-
-    lower_start = lax.rem(me_a + area_size - 1, area_size) * span
-    window = gains_of(lower_start, me_a > 0) + gains_of(first, me_a >= 0)
-
-    for copy in coup_copies:
-        copy.wait()
-    coupling = [coup_halo[0, i : i + 1, :] for i in range(span)]
-    coupling += [coup_ref[i : i + 1, :] for i in range(span)]
-    coupling += [coup_halo[1, i : i + 1, :] for i in range(span)]
     offsets = [o for o in range(-TIES, TIES + 1) if o != 0]
-    for i in range(span):
-        total = 2.0 * ramp_ref[i : i + 1, :]
-        for k, o in enumerate(offsets):
-            gain = window[span + i][o - 1] if o > 0 else window[span + i + o][-o - 1]
-            row = coupling[span + i] * coupling[span + i + o] * gain
-            tie_buf[i, k : k + 1, :] = row
-            total = total + row
-        diag_buf[i] = diag_buf[i] + total
 
     def tile_part(value, i):
         high, low = split(value)
@@ -336,10 +323,6 @@
     pieces_three = [(0, 3), (1, 0)]
     pieces_four = [(0, 0), (1, 3)]
 
-    for i in range(span):
-        acc[i] = tile_part(guess_ref[i], i)
-        near_part(guess_ref, i)
-
     group = plane * per_device
     passes, relays = [], []
 
@@ -356,7 +339,7 @@
         copy.start()
         relays.append(copy)
 
-    for k in range(zeds):
+    def go_round(k):
         for e in range(plane):
             key = steps[k] * plane + e
             if key == 0:
@@ -373,7 +356,39 @@
         passes.append(pair)
         if k >= 1:
             relay(k - 1)
+
+    go_round(0)
+    go_round(1)
+    for copy in coup_copies:
+        copy.wait()
+    coupling = [coup_halo[0, i : i + 1, :] for i in range(span)]
+    coupling += [coup_ref[i : i + 1, :] for i in range(span)]
+    coupling += [coup_halo[1, i : i + 1, :] for i in range(span)]
+    for i in range(span):
+        total = 2.0 * ramp_ref[i : i + 1, :]
+        for k, o in enumerate(offsets):
+            gain = window[span + i][o - 1] if o > 0 else window[span + i + o][-o - 1]
+            row = coupling[span + i] * coupling[span + i + o] * gain
+            tie_buf[i, k : k + 1, :] = row
+            total = total + row
+        diag_buf[i] = diag_buf[i] + total
+
+    go_round(2)
+    acc[0] = tile_part(guess_ref[0], 0)
+    near_part(guess_ref, 0)
+    go_round(3)
+    acc[1] = tile_part(guess_ref[1], 1)
+    near_part(guess_ref, 1)
+    go_round(4)
+    acc[2] = tile_part(guess_ref[2], 2)
+    near_part(guess_ref, 2)
+    go_round(5)
+    acc[3] = tile_part(guess_ref[3], 3)
+    near_part(guess_ref, 3)
+    go_round(6)
+    go_round(7)
     relay(zeds - 1)
+
     for key, copy in load_copies.items():
         if key == 0:
             copy.wait()
@@ -530,6 +545,11 @@
             copy.wait_send()
 
 
+def deliver(step_ref, resid_ref, step_out, resid_out):
+    step_out[...] = step_ref[...]
+    resid_out[...] = resid_ref[...]
+
+
 def body(
     gradient, barrier, slack, hess_diag, tile, ramp_weight, bus_coupling, tie_offset, tie_admittance,
     con_sens, con_weight, con_owner, step_guess,
@@ -586,6 +606,9 @@
         barrier, tie_offset.T, tie_admittance.T, rows_of(slack), rows_of(hess_diag), rows_of(gradient),
         rows_of(step_guess), tile, ramp_weight, bus_coupling, con_sens, con_weight.T, con_owner.T,
     )
+    step, residual = pl.pallas_call(
+        deliver, out_shape=(flat, flat), in_specs=[vmem, vmem], out_specs=(vmem, vmem),
+    )(step, residual)
     return field_of(step), field_of(residual)
 
 

time: 79.1 us -> 72.9 us (0.922)
  local copies, waits for them, and re-layouts: 3.46 us -> 0 us
  Pallas kernels: 74.1 us -> 71.4 us
    pallas_call x1, Pallas kernels: 74.1 us -> 69.5 us  [body(): pl.pallas_call(functools.partial(kernel, hours, tm_size, area_size), out_...]
    unnamed x2 -> x0, local copies, waits for them, and re-layouts: 3.46 us -> none
    pallas_call x0 -> x1, Pallas kernels: none -> 1.95 us  [body(): pl.pallas_call(deliver, out_shape=(flat, flat), in_specs=[vmem, vmem], ou...]
where the time goes in v3:
time: 72.9 us; the launch traced here: 72.7 us
  Pallas kernels  71.4 us (98%)
  between operations  1.29 us (2%)
    pallas_call x1, Pallas kernels, body(): pl.pallas_call(functools.partial(kernel, hours, tm_size, area_size), out_...  69.5 us
    pallas_call x1, Pallas kernels, body(): pl.pallas_call(deliver, out_shape=(flat, flat), in_specs=[vmem, vmem], ou...  1.95 us

profile of v3, /device:TPU:1, one launch (start us, length us, event | category | flops | bytes accessed | tf_op | source)
XLA Modules:
  0.0 72.7 jit_solution(12380819912785200525)
XLA Ops:
  1.3 69.5 %shard_map.140 = (f32[672,128]{1,0:T(8,128)}, f32[672,128]{1,0:T(8,128)}) custom-call(f32[1]{0:T(128)S(6)} %copy.21.barrier_ref, s32[4,256]{1,0:T(4,128)} %bitcast.39, f32[4,256]{1,0:T(4,128)} %bitcast.40, f32[672,128]{1,0:T(8,128)} %bitcast.34, f32[672,128]{1,0:T(8,128)} %bitcast.35, f32[672,128]{1,0:T(8,128)} %bitcast.36, f32[672,128]{1,0:T(8,128)} %bitcast.37, ...), custom_call_target="tpu_custom_call" | custom-call | tf_op jit(solution)/shard_map/pallas_call | solution.py:579
  70.7 1.9 %shard_map.141 = (f32[672,128]{1,0:T(8,128)}, f32[672,128]{1,0:T(8,128)}) custom-call(f32[672,128]{1,0:T(8,128)} %get-tuple-element.6.step_ref, f32[672,128]{1,0:T(8,128)} %get-tuple-element.7.resid_ref), custom_call_target="tpu_custom_call" | custom-call | tf_op jit(solution)/shard_map/pallas_call | solution.py:609
